TPU v7x, 32 devices: a whole 2x2x4 slice. The times are simulated.
32 devices in a mesh: row: 8 (over y, x, core), col: 4 (over z).
Axes of the slice: x: 2, y: 2, z: 4, core: 2. Of those that a mesh axis runs over, the one named last changes fastest.
Arguments:
- trials: float32 [2, 512, 1024], P(None, 'col', 'row'), may hold values from -6 to 6
- valence_factor: float32 [16384, 512], P('row'), may hold values from -0.25 to 0.25
- conduction_factor: float32 [16384, 1024], P('col', 'row'), may hold values from -0.046875 to 0.046875
- screened: float32 [16384, 16384], P('row', 'col'), may hold values from -6 to 6
- valence_energy: float32 [512], P('col'), may hold values from -0.6 to -0.1
- conduction_energy: float32 [1024], P('row'), may hold values from 0.1 to 0.6
Outputs:
- applied: float32 [2, 512, 1024], P(None, 'col', 'row')
All inputs are finite; a program needn't handle non-finite values.
Results may differ from a plain program's by a relative error of at most 0.0001.
Values sent between devices are 32-bit elements; how exact they have to be, the bound alone decides.
A program may use at most 256 MiB of HBM per device.

v0:
```python
import jax
import jax.numpy as jnp
from jax import lax
from jax.sharding import PartitionSpec as P


def body(trials, valence_factor, conduction_factor, screened, valence_energy, conduction_energy):
    highest = lax.Precision.HIGHEST
    all_valence = lax.all_gather(trials, "col", axis=1, tiled=True)
    partial_value = jnp.einsum("bvc,nc->bvn", all_valence, conduction_factor, precision=highest)
    points = lax.psum(partial_value, "row")
    expanded = jnp.einsum("mv,bvn->bmn", valence_factor, points, precision=highest)
    weighted = expanded * screened[None]
    folded = jnp.einsum("mv,bmn->bvn", valence_factor, weighted, precision=highest)
    shares = lax.psum_scatter(folded, "row", scatter_dimension=1, tiled=True)
    factor_full = lax.all_gather(conduction_factor, "row", axis=1, tiled=True)
    kernel_rows = jnp.einsum("bvn,nc->bvc", shares, factor_full, precision=highest)
    swapped = lax.all_to_all(kernel_rows, "row", split_axis=2, concat_axis=1, tiled=True)
    kernel_term = lax.psum_scatter(swapped, "col", scatter_dimension=1, tiled=True)
    differences = conduction_energy[None, :] - valence_energy[:, None]
    return differences[None] * trials - kernel_term


def solution(mesh):
    in_specs = (
        P(None, "col", "row"),
        P("row", None),
        P("col", "row"),
        P("row", "col"),
        P("col"),
        P("row"),
    )
    out_specs = P(None, "col", "row")
    return jax.shard_map(body, mesh=mesh, in_specs=in_specs, out_specs=out_specs, check_vma=False)
```

profile of v0, /device:TPU:0, one launch (start us, length us, event | category | flops | bytes accessed | tf_op | source)
XLA Modules:
  0.0 781.5 jit_solution(15031919599068699911)
XLA Ops:
  6.5 0.0 all-reduce.2.cloned.1.call-start
  6.5 17.6 %all_gather.6 = f32[2,512,128]{2,1,0:T(8,128)S(1)} all-gather(f32[2,128,128]{2,1,0:T(8,128)} %param.6), channel_id=1, replica_groups=mesh['row'=8,'col'=4] {'col'}, dimensions={1}, use_global_device_ids=true | all-gather | bytes 655360 | tf_op jit(solution)/shard_map/all_gather | solution.py:9
  24.1 16.8 %fusion.8 = f32[2,512,4096]{2,1,0:T(8,128)} fusion(f32[2,512,128]{2,1,0:T(8,128)S(1)} %all_gather.6, f32[4096,128]{1,0:T(8,128)} %param.8), kind=kOutput, calls=%fused_computation.9 | convolution fusion | flops 6442450944 | bytes 19398656 | tf_op jit(solution)/shard_map/bvc,nc->bvn/dot_general | solution.py:10
  40.9 0.0 all-reduce.2.cloned.1.call-update
  40.9 0.0 all-gather.2.cloned.1.call-start
  41.0 0.7 all-gather.2.cloned.1.call-update
  41.7 0.0 reduce-scatter.3.cloned.1.call-start
  41.7 33.8 %copy.9 = f32[2048,4096]{0,1:T(8,128)} copy(f32[2048,4096]{1,0:T(8,128)} %param.9) | data formatting | bytes 67108864 | tf_op args[3]
  75.5 185.1 %all-reduce.2.cloned.1.call-done = f32[2,512,4096]{2,1,0:T(8,128)} async-done(((f32[2,512,4096]{2,1,0:T(8,128)}), f32[2,512,4096]{2,1,0:T(8,128)}) %all-reduce.2.cloned.1.call-update) | async-done | bytes 16777232 | tf_op jit(solution)/shard_map/psum | solution.py:11
  260.6 0.0 copy-start
  260.6 217.2 %fusion.6 = f32[2,4096,2048]{2,1,0:T(8,128)} fusion(f32[2,512,4096]{2,1,0:T(8,128)} %all-reduce.2.cloned.1.call-done, f32[2048,512]{1,0:T(8,128)} %param.7), kind=kOutput, calls=%fused_computation.7 | convolution fusion | flops 103079215104 | bytes 88080384 | tf_op jit(solution)/shard_map/mv,bvn->bmn/dot_general | solution.py:12
  477.8 0.0 copy-done
  477.8 125.9 %fusion.4 = f32[2,512,4096]{2,1,0:T(8,128)} fusion(f32[2,4096,2048]{2,1,0:T(8,128)} %fusion.6, f32[2048,4096]{0,1:T(8,128)} %copy.9, f32[2048,512]{1,0:T(8,128)S(1)} %copy-done), kind=kOutput, calls=%fused_computation.5 | convolution fusion | flops 103095992320 | bytes 121634816 | tf_op jit(solution)/shard_map/mv,bmn->bvn/dot_general | solution.py:14
  603.7 0.0 reduce-scatter.3.cloned.1.call-update
  603.8 0.0 copy-start.2
  603.8 0.0 copy-start.3
  603.8 0.0 copy-start.1
  603.8 0.0 reduce-scatter.5.cloned.1.call-start
  603.9 0.0 all-gather.2.cloned.1.call-done
  603.9 116.3 %reduce-scatter.3.cloned.1.call-done = f32[2,64,4096]{2,1,0:T(8,128)} async-done(((f32[2,512,4096]{2,1,0:T(8,128)}), f32[2,64,4096]{2,1,0:T(8,128)}) %reduce-scatter.3.cloned.1.call-update) | async-done | bytes 2097168 | tf_op jit(solution)/shard_map/reduce_scatter | solution.py:15
  720.1 13.6 %fusion.2 = f32[2,64,1024]{2,1,0:T(8,128)S(1)} fusion(f32[2,64,4096]{2,1,0:T(8,128)} %reduce-scatter.3.cloned.1.call-done, f32[4096,1024]{1,0:T(8,128)} %all-gather.2.cloned.1.call-done), kind=kOutput, calls=%fused_computation.3 | convolution fusion | flops 6442450944 | bytes 19398656 | tf_op jit(solution)/shard_map/bvn,nc->bvc/dot_general | solution.py:17
  733.7 0.6 copy.10
  734.3 1.1 reshape.31
  735.4 12.2 %all_to_all.18 = f32[8,1,16384]{2,1,0:T(1,128)S(1)} all-to-all(f32[8,1,16384]{2,1,0:T(1,128)S(1)} %reshape.31), channel_id=1, replica_groups=mesh['row'=8,'col'=4] {'row'}, dimensions={0} | all-to-all | bytes 1048576 | tf_op jit(solution)/shard_map/all_to_all | solution.py:18
  747.6 0.5 broadcast.20
  748.1 1.9 reduce
  750.0 0.8 reshape.32
  750.8 1.2 copy.11
  752.0 0.0 reduce-scatter.5.cloned.1.call-update
  752.0 0.0 copy-done.2
  752.0 0.0 copy-done.3
  752.0 0.1 broadcast_subtract_fusion
  752.1 21.0 %reduce-scatter.5.cloned.1.call-done = f32[2,128,128]{2,1,0:T(8,128)} async-done(((f32[2,512,128]{2,1,0:T(8,128)}), f32[2,128,128]{2,1,0:T(8,128)}) %reduce-scatter.5.cloned.1.call-update) | async-done | bytes 131088 | tf_op jit(solution)/shard_map/reduce_scatter | solution.py:19
  773.1 0.0 copy-done.1
  773.1 1.6 multiply_subtract_fusion
Async XLA Ops:
  6.5 254.1 %all-reduce.2.cloned.1.call-start = ((), (), s32[]{:S(2)}) async-start(), calls=%async_computation.3 | async-start | bytes 33554432 | tf_op jit(solution)/shard_map/psum | solution.py:11
  40.9 563.0 %all-gather.2.cloned.1.call-start = ((), (), s32[]{:S(2)}) async-start(), calls=%async_computation.5 | async-start | bytes 18874368 | tf_op jit(solution)/shard_map/all_gather | solution.py:16
  41.7 678.5 %reduce-scatter.3.cloned.1.call-start = ((), (), s32[]{:S(2)}) async-start(), calls=%async_computation.4 | async-start | bytes 18874368 | tf_op jit(solution)/shard_map/reduce_scatter | solution.py:15
  260.6 217.2 %copy-start = (f32[2048,512]{1,0:T(8,128)S(1)}, f32[2048,512]{1,0:T(8,128)}, u32[]{:S(2)}) copy-start(f32[2048,512]{1,0:T(8,128)} %param.7) | copy-start | bytes 12582916
  603.8 148.2 %copy-start.2 = (f32[128]{0:T(128)S(1)}, f32[128]{0:T(128)}, u32[]{:S(2)}) copy-start(f32[128]{0:T(128)} %param.10) | copy-start | bytes 1540
  603.8 148.2 %copy-start.3 = (f32[128]{0:T(128)S(1)}, f32[128]{0:T(128)}, u32[]{:S(2)}) copy-start(f32[128]{0:T(128)} %param.11) | copy-start | bytes 1540
  603.8 169.3 %copy-start.1 = (f32[2,128,128]{2,1,0:T(8,128)S(1)}, f32[2,128,128]{2,1,0:T(8,128)}, u32[]{:S(2)}) copy-start(f32[2,128,128]{2,1,0:T(8,128)} %param.6) | copy-start | bytes 393220
  603.8 169.3 %reduce-scatter.5.cloned.1.call-start = ((), (), s32[]{:S(2)}) async-start(), calls=%async_computation.6 | async-start | bytes 655360 | tf_op jit(solution)/shard_map/reduce_scatter | solution.py:19
Sparse Core Ops, SparseCore 0:
  41.0 219.5 all-reduce.1
  262.5 93.0 all-gather.1
  603.9 116.1 reduce-scatter.2
  752.1 20.9 reduce-scatter.4
where the time goes:
time: 786 us; the launch traced here: 781 us
  matrix products  373 us (47%)
  waiting for transfers between devices  323 us (41%)
  local copies, waits for them, and re-layouts  38 us (5%)
  blocking collectives  29.8 us (4%)
  between operations  13.4 us (2%)
    dot_general x1, matrix products, body(): jnp.einsum('mv,bvn->bmn', valence_factor, points, precision=highest)  217 us
    psum x1, waiting for transfers between devices, body(): points = lax.psum(partial_value, 'row')  185 us
    dot_general x1, matrix products, body(): jnp.einsum('mv,bmn->bvn', valence_factor, weighted, precision=highest)  126 us
    reduce_scatter x1, waiting for transfers between devices, body(): shares = lax.psum_scatter(folded, 'row', scatter_dimension=1, tiled=True)  116 us
    unnamed x11, local copies, waits for them, and re-layouts  35.7 us
    reduce_scatter x1, waiting for transfers between devices, body(): lax.psum_scatter(swapped, 'col', scatter_dimension=1, tiled=True)  21 us
    all_gather x1, blocking collectives, body(): all_valence = lax.all_gather(trials, 'col', axis=1, tiled=True)  17.6 us
    dot_general x1, matrix products, body(): jnp.einsum('bvc,nc->bvn', all_valence, conduction_factor, precision=highest)  16.8 us
  transfers between devices with their start and end apart: 4, of which 3 were waited for; matrix products, arithmetic and copies ran while one was open for 48% of the time, Pallas kernels for 0%

commit v1 on v0

--- a/solution.py
+++ b/solution.py
@@ -4,11 +4,20 @@
 from jax.sharding import PartitionSpec as P
 
 
+def add_in_pairs(x, axis):
+    size = lax.axis_size(axis)
+    total, far = (x, 1)
+    while far < size:
+        total = total + lax.ppermute(total, axis, [(i, i ^ far) for i in range(size)])
+        far = 2 * far
+    return total
+
+
 def body(trials, valence_factor, conduction_factor, screened, valence_energy, conduction_energy):
     highest = lax.Precision.HIGHEST
     all_valence = lax.all_gather(trials, "col", axis=1, tiled=True)
     partial_value = jnp.einsum("bvc,nc->bvn", all_valence, conduction_factor, precision=highest)
-    points = lax.psum(partial_value, "row")
+    points = add_in_pairs(partial_value, "row")
     expanded = jnp.einsum("mv,bvn->bmn", valence_factor, points, precision=highest)
     weighted = expanded * screened[None]
     folded = jnp.einsum("mv,bmn->bvn", valence_factor, weighted, precision=highest)

time: 786 us -> 1410 us (1.79)
  waiting for transfers between devices: 323 us -> 920 us
  other arithmetic: 3.54 us -> 33.2 us
    ppermute x0 -> x3, waiting for transfers between devices: none -> 781 us  [add_in_pairs(): lax.ppermute(total, axis, [(i, i ^ far) for i in range(size)])]
    psum x1 -> x0, waiting for transfers between devices: 185 us -> none  [body(): points = lax.psum(partial_value, 'row')]
    add x0 -> x2, other arithmetic: none -> 29.6 us  [add_in_pairs(): total + lax.ppermute(total, axis, [(i, i ^ far) for i in range(size)])]
  transfers between devices with their start and end apart: 4 -> 6, of which waited for: 3 -> 5; matrix products, arithmetic and copies ran while one was open for 48% -> 28% of each run, Pallas kernels for 0% -> 0%
where the time goes in v1:
time: 1410 us; the launch traced here: 1400 us
  waiting for transfers between devices  920 us (65%)
  matrix products  363 us (26%)
  local copies, waits for them, and re-layouts  37.5 us (3%)
  other arithmetic  33.2 us (2%)
  blocking collectives  29.8 us (2%)
    ppermute x3, waiting for transfers between devices, add_in_pairs(): lax.ppermute(total, axis, [(i, i ^ far) for i in range(size)])  781 us
    dot_general x1, matrix products, body(): jnp.einsum('mv,bvn->bmn', valence_factor, points, precision=highest)  218 us
    reduce_scatter x1, waiting for transfers between devices, body(): shares = lax.psum_scatter(folded, 'row', scatter_dimension=1, tiled=True)  118 us
    dot_general x1, matrix products, body(): jnp.einsum('mv,bmn->bvn', valence_factor, weighted, precision=highest)  116 us
    unnamed x11, local copies, waits for them, and re-layouts  35.3 us
    add x2, other arithmetic, add_in_pairs(): total + lax.ppermute(total, axis, [(i, i ^ far) for i in range(size)])  29.6 us
  transfers between devices with their start and end apart: 6, of which 5 were waited for; matrix products, arithmetic and copies ran while one was open for 28% of the time, Pallas kernels for 0%

profile of v1, /device:TPU:0, one launch (start us, length us, event | category | flops | bytes accessed | tf_op | source)
XLA Modules:
  0.0 1399.9 jit_solution(5850280088801633028)
XLA Ops:
  6.5 0.0 all-gather.2.cloned.1.call-start
  6.5 17.6 %all_gather.6 = f32[2,512,128]{2,1,0:T(8,128)S(1)} all-gather(f32[2,128,128]{2,1,0:T(8,128)} %param.6), channel_id=1, replica_groups=mesh['row'=8,'col'=4] {'col'}, dimensions={1}, use_global_device_ids=true | all-gather | bytes 655360 | tf_op jit(solution)/shard_map/all_gather | solution.py:18
  24.1 15.0 %fusion.9 = f32[2,512,4096]{2,1,0:T(8,128)S(1)} fusion(f32[2,512,128]{2,1,0:T(8,128)S(1)} %all_gather.6, f32[4096,128]{1,0:T(8,128)} %param.8), kind=kOutput, calls=%fused_computation.10 | convolution fusion | flops 6442450944 | bytes 19398656 | tf_op jit(solution)/shard_map/bvc,nc->bvn/dot_general | solution.py:19
  39.1 0.1 collective-permute-start
  39.2 25.3 %collective-permute-done = f32[2,512,4096]{2,1,0:T(8,128)} collective-permute-done((f32[2,512,4096]{2,1,0:T(8,128)S(1)}, f32[2,512,4096]{2,1,0:T(8,128)}, u32[]{:S(2)}, u32[]{:S(2)}) %collective-permute-start) | collective-permute-done | bytes 16777248 | tf_op jit(solution)/shard_map/ppermute | solution.py:11
  64.5 11.8 add.13
  76.3 1.5 collective-permute-start.1
  77.8 0.0 all-gather.2.cloned.1.call-update
  77.8 0.0 reduce-scatter.3.cloned.1.call-start
  77.9 428.4 %collective-permute-done.1 = f32[2,512,4096]{2,1,0:T(8,128)} collective-permute-done((f32[2,512,4096]{2,1,0:T(8,128)}, f32[2,512,4096]{2,1,0:T(8,128)}, u32[]{:S(2)}, u32[]{:S(2)}) %collective-permute-start.1) | collective-permute-done | bytes 16777248 | tf_op jit(solution)/shard_map/ppermute | solution.py:11
  506.3 17.8 %add.14 = f32[2,512,4096]{2,1,0:T(8,128)} add(f32[2,512,4096]{2,1,0:T(8,128)} %add.13, f32[2,512,4096]{2,1,0:T(8,128)} %collective-permute-done.1) | non-fusion elementwise | flops 4194304 | bytes 50331648 | tf_op jit(solution)/shard_map/add | solution.py:11
  524.1 1.5 collective-permute-start.2
  525.6 33.4 %copy.9 = f32[2048,4096]{0,1:T(8,128)} copy(f32[2048,4096]{1,0:T(8,128)} %param.9) | data formatting | bytes 67108864 | tf_op args[3]
  559.0 0.0 copy-start
  559.0 326.8 %collective-permute-done.2 = f32[2,512,4096]{2,1,0:T(8,128)} collective-permute-done((f32[2,512,4096]{2,1,0:T(8,128)}, f32[2,512,4096]{2,1,0:T(8,128)}, u32[]{:S(2)}, u32[]{:S(2)}) %collective-permute-start.2) | collective-permute-done | bytes 16777248 | tf_op jit(solution)/shard_map/ppermute | solution.py:11
  885.8 218.3 %fusion.4 = f32[2,4096,2048]{2,1,0:T(8,128)} fusion(f32[2,512,4096]{2,1,0:T(8,128)} %add.14, f32[2,512,4096]{2,1,0:T(8,128)} %collective-permute-done.2, f32[2048,512]{1,0:T(8,128)} %param.7), kind=kOutput, calls=%fused_computation.5 | convolution fusion | flops 103083409408 | bytes 104857600 | tf_op jit(solution)/shard_map/mv,bvn->bmn/dot_general | solution.py:21
  1104.1 0.0 copy-done
  1104.1 116.3 %fusion.6 = f32[2,512,4096]{2,1,0:T(8,128)} fusion(f32[2,4096,2048]{2,1,0:T(8,128)} %fusion.4, f32[2048,4096]{0,1:T(8,128)} %copy.9, f32[2048,512]{1,0:T(8,128)S(1)} %copy-done), kind=kOutput, calls=%fused_computation.7 | convolution fusion | flops 103095992320 | bytes 121634816 | tf_op jit(solution)/shard_map/mv,bmn->bvn/dot_general | solution.py:23
  1220.4 0.0 reduce-scatter.3.cloned.1.call-update
  1220.5 0.0 copy-start.2
  1220.5 0.0 copy-start.3
  1220.5 0.0 copy-start.1
  1220.5 0.0 reduce-scatter.5.cloned.1.call-start
  1220.5 0.0 all-gather.2.cloned.1.call-done
  1220.6 118.0 %reduce-scatter.3.cloned.1.call-done = f32[2,64,4096]{2,1,0:T(8,128)} async-done(((f32[2,512,4096]{2,1,0:T(8,128)}), f32[2,64,4096]{2,1,0:T(8,128)}) %reduce-scatter.3.cloned.1.call-update) | async-done | bytes 2097168 | tf_op jit(solution)/shard_map/reduce_scatter | solution.py:24
  1338.6 13.6 fusion.2
  1352.2 0.6 copy.10
  1352.7 1.1 reshape.31
  1353.8 12.3 all_to_all.18
  1366.1 0.5 broadcast.20
  1366.6 1.9 reduce
  1368.5 0.8 reshape.32
  1369.3 1.2 copy.11
  1370.4 0.0 reduce-scatter.5.cloned.1.call-update
  1370.5 0.0 copy-done.2
  1370.5 0.0 copy-done.3
  1370.5 0.1 broadcast_subtract_fusion
  1370.6 21.0 %reduce-scatter.5.cloned.1.call-done = f32[2,128,128]{2,1,0:T(8,128)} async-done(((f32[2,512,128]{2,1,0:T(8,128)}), f32[2,128,128]{2,1,0:T(8,128)}) %reduce-scatter.5.cloned.1.call-update) | async-done | bytes 131088 | tf_op jit(solution)/shard_map/reduce_scatter | solution.py:28
  1391.6 0.0 copy-done.1
  1391.6 1.6 multiply_subtract_fusion
Async XLA Ops:
  6.5 1214.0 %all-gather.2.cloned.1.call-start = ((), (), s32[]{:S(2)}) async-start(), calls=%async_computation.4 | async-start | bytes 18874368 | tf_op jit(solution)/shard_map/all_gather | solution.py:25
  39.1 25.4 %collective-permute-start = (f32[2,512,4096]{2,1,0:T(8,128)S(1)}, f32[2,512,4096]{2,1,0:T(8,128)}, u32[]{:S(2)}, u32[]{:S(2)}) collective-permute-start(f32[2,512,4096]{2,1,0:T(8,128)S(1)} %fusion.9), channel_id=1, source_target_pairs={{0,4},{4,0},{8,12},{12,8},{16,20},{20,16},{24,28},{28,24},{1,5},{5... | collective-permute-start | bytes 50331656 | tf_op jit(solution)/shard_map/ppermute | solution.py:11
  76.3 430.0 %collective-permute-start.1 = (f32[2,512,4096]{2,1,0:T(8,128)}, f32[2,512,4096]{2,1,0:T(8,128)}, u32[]{:S(2)}, u32[]{:S(2)}) collective-permute-start(f32[2,512,4096]{2,1,0:T(8,128)} %add.13), channel_id=1, source_target_pairs={{0,8},{4,12},{8,0},{12,4},{16,24},{20,28},{24,16},{28,20},{1,9},{5... | collective-permute-start | bytes 50331656 | tf_op jit(solution)/shard_map/ppermute | solution.py:11
  77.8 1260.7 %reduce-scatter.3.cloned.1.call-start = ((), (), s32[]{:S(2)}) async-start(), calls=%async_computation.3 | async-start | bytes 18874368 | tf_op jit(solution)/shard_map/reduce_scatter | solution.py:24
  524.1 361.7 %collective-permute-start.2 = (f32[2,512,4096]{2,1,0:T(8,128)}, f32[2,512,4096]{2,1,0:T(8,128)}, u32[]{:S(2)}, u32[]{:S(2)}) collective-permute-start(f32[2,512,4096]{2,1,0:T(8,128)} %add.14), channel_id=1, source_target_pairs={{0,16},{4,20},{8,24},{12,28},{16,0},{20,4},{24,8},{28,12},{1,17},{... | collective-permute-start | bytes 50331656 | tf_op jit(solution)/shard_map/ppermute | solution.py:11
  559.0 545.1 %copy-start = (f32[2048,512]{1,0:T(8,128)S(1)}, f32[2048,512]{1,0:T(8,128)}, u32[]{:S(2)}) copy-start(f32[2048,512]{1,0:T(8,128)} %param.7) | copy-start | bytes 12582916
  1220.5 150.0 %copy-start.2 = (f32[128]{0:T(128)S(1)}, f32[128]{0:T(128)}, u32[]{:S(2)}) copy-start(f32[128]{0:T(128)} %param.10) | copy-start | bytes 1540
  1220.5 150.0 %copy-start.3 = (f32[128]{0:T(128)S(1)}, f32[128]{0:T(128)}, u32[]{:S(2)}) copy-start(f32[128]{0:T(128)} %param.11) | copy-start | bytes 1540
  1220.5 171.1 %copy-start.1 = (f32[2,128,128]{2,1,0:T(8,128)S(1)}, f32[2,128,128]{2,1,0:T(8,128)}, u32[]{:S(2)}) copy-start(f32[2,128,128]{2,1,0:T(8,128)} %param.6) | copy-start | bytes 393220
  1220.5 171.1 %reduce-scatter.5.cloned.1.call-start = ((), (), s32[]{:S(2)}) async-start(), calls=%async_computation.5 | async-start | bytes 655360 | tf_op jit(solution)/shard_map/reduce_scatter | solution.py:28
Sparse Core Ops, SparseCore 0:
  77.9 157.9 all-gather.1
  1220.6 117.9 reduce-scatter.2
  1370.6 20.9 reduce-scatter.4
